TPU v7x, 32 devices: a whole 2x2x4 slice. The times are simulated.
32 devices in a mesh: dp: 8 (over z, x), seq: 4 (over y, core).
Axes of the slice: x: 2, y: 2, z: 4, core: 2. Of those that a mesh axis runs over, the one named last changes fastest.
Arguments:
- captions: bfloat16 [96, 128, 768], P(('dp', 'seq')), may hold values from -6 to 6
- images: bfloat16 [96, 196, 768], P('dp'), may hold values from -6 to 6
- tissue_mask: int32 [96, 196], P('dp'), may hold values from 0 to 1, as said below
- gain_self: bfloat16 [768], P(('dp', 'seq')), may hold values from 0.5 to 1.5
- gain_cross: bfloat16 [768], P(('dp', 'seq')), may hold values from 0.5 to 1.5
- gain_mlp: bfloat16 [768], P(('dp', 'seq')), may hold values from 0.5 to 1.5
- w_qkv: bfloat16 [768, 2304], P(('dp', 'seq')), may hold values from -0.21875 to 0.21875
- w_self_out: bfloat16 [768, 768], P(('dp', 'seq')), may hold values from -0.625 to 0.625
- w_cross_q: bfloat16 [768, 768], P(('dp', 'seq')), may hold values from -0.21875 to 0.21875
- w_cross_kv: bfloat16 [768, 1536], P(('dp', 'seq')), may hold values from -0.21875 to 0.21875
- w_cross_out: bfloat16 [768, 768], P(('dp', 'seq')), may hold values from -0.625 to 0.625
- w_up: bfloat16 [768, 3072], P(('dp', 'seq')), may hold values from -0.21875 to 0.21875
- w_down: bfloat16 [3072, 768], P(('dp', 'seq')), may hold values from -0.109375 to 0.109375
- cotangent: bfloat16 [96, 128, 768], P(('dp', 'seq')), may hold values from -6 to 6
Outputs:
- block_out: bfloat16 [96, 128, 768], P(('dp', 'seq'))
- grad_captions: float32 [96, 128, 768], P(('dp', 'seq'))
- grad_images: float32 [96, 196, 768], P('dp', None, 'seq')
- grad_gain_self: float32 [768], P(('dp', 'seq'))
- grad_gain_cross: float32 [768], P(('dp', 'seq'))
- grad_gain_mlp: float32 [768], P(('dp', 'seq'))
- grad_w_qkv: float32 [768, 2304], P(('dp', 'seq'))
- grad_w_self_out: float32 [768, 768], P(('dp', 'seq'))
- grad_w_cross_q: float32 [768, 768], P(('dp', 'seq'))
- grad_w_cross_kv: float32 [768, 1536], P(('dp', 'seq'))
- grad_w_cross_out: float32 [768, 768], P(('dp', 'seq'))
- grad_w_up: float32 [768, 3072], P(('dp', 'seq'))
- grad_w_down: float32 [3072, 768], P(('dp', 'seq'))
Inputs may be any that keep to these rules, and one draw needn't show every extreme that they name: `tissue_mask`: at least 65 of every image's patches are valid; the valid ones lie anywhere among its 196 slots and their number differs from image to image.
All inputs are finite; a program needn't handle non-finite values.
Results may differ from a plain program's by a relative error of at most 0.019.
Values may be sent and summed in bfloat16 or wider, within the bound.
A program may use at most 192 MiB of HBM per device.

v0:
```python
import jax
import jax.numpy as jnp
from jax import lax
from jax.sharding import PartitionSpec as P

HEADS = 12
HEAD = 64


epsilon = 1e-05


def layer_norm(inputs, gain_vector):
    centered = inputs - jnp.mean(inputs, axis=-1, keepdims=True)
    spread = jnp.mean(centered * centered, axis=-1, keepdims=True)
    return centered * lax.rsqrt(spread + epsilon) * gain_vector


def norm_back(inputs, gain_vector, upstream):
    unused, pullback = jax.vjp(layer_norm, inputs, gain_vector)
    return pullback(upstream)


def exact_gelu(inputs):
    return jax.nn.gelu(inputs, approximate=False)


def linear(inputs, matrix):
    return jnp.einsum("btd,de->bte", inputs, matrix, preferred_element_type=jnp.float32)


def linear_back(upstream, matrix):
    return jnp.einsum("bte,de->btd", upstream, matrix, preferred_element_type=jnp.float32)


def weight_grad(inputs, upstream):
    return jnp.einsum("btd,bte->de", inputs, upstream, preferred_element_type=jnp.float32)


def masked_scores(query_heads, key_heads, allowed, factor):
    raw_scores = (
        jnp.einsum("bqhe,bkhe->bhqk", query_heads, key_heads, preferred_element_type=jnp.float32)
        * factor
    )
    return jnp.where(allowed, raw_scores, -1e30)


def attend_forward(query_heads, key_heads, value_heads, allowed, factor):
    scores = masked_scores(query_heads, key_heads, allowed, factor)
    top_score = jnp.max(scores, axis=-1, keepdims=True)
    exponent = jnp.exp(scores - top_score)
    totals = jnp.sum(exponent, axis=-1, keepdims=True)
    probabilities = (exponent / totals).astype(jnp.bfloat16)
    attended = jnp.einsum(
        "bhqk,bkhe->bqhe", probabilities, value_heads, preferred_element_type=jnp.float32
    )
    return (attended.astype(jnp.bfloat16), top_score + jnp.log(totals))


def attend_back(query_heads, key_heads, value_heads, allowed, factor, log_totals, upstream):
    probabilities = jnp.exp(masked_scores(query_heads, key_heads, allowed, factor) - log_totals)
    grad_probs = jnp.einsum(
        "bqhe,bkhe->bhqk", upstream, value_heads, preferred_element_type=jnp.float32
    )
    centered = grad_probs - jnp.sum(grad_probs * probabilities, axis=-1, keepdims=True)
    grad_scores = (probabilities * centered * factor).astype(jnp.bfloat16)
    grad_queries = jnp.einsum(
        "bhqk,bkhe->bqhe", grad_scores, key_heads, preferred_element_type=jnp.float32
    )
    grad_keys = jnp.einsum(
        "bhqk,bqhe->bkhe", grad_scores, query_heads, preferred_element_type=jnp.float32
    )
    grad_values = jnp.einsum(
        "bhqk,bqhe->bkhe",
        probabilities.astype(jnp.bfloat16),
        upstream,
        preferred_element_type=jnp.float32,
    )
    return (
        grad_queries.astype(jnp.bfloat16),
        grad_keys.astype(jnp.bfloat16),
        grad_values.astype(jnp.bfloat16),
    )


def pair_columns(full_cross_kv, seq_index, head_span, model_width):
    key_cols = lax.dynamic_slice_in_dim(full_cross_kv, seq_index * head_span, head_span, 1)
    value_cols = lax.dynamic_slice_in_dim(
        full_cross_kv, model_width + seq_index * head_span, head_span, 1
    )
    return jnp.concatenate([key_cols, value_cols], axis=1)


def on_device(
    captions,
    images,
    tissue_mask,
    gain_self,
    gain_cross,
    gain_mlp,
    w_qkv,
    w_self_out,
    w_cross_q,
    w_cross_kv,
    w_cross_out,
    w_up,
    w_down,
    cotangent,
):
    groups = lax.axis_size("seq")
    seq_index = lax.axis_index("seq")
    count_local, full_len, model_width = captions.shape
    count_caps = count_local * groups
    patch_count = images.shape[1]
    local_heads = HEADS // groups
    head_span = local_heads * HEAD
    factor = HEAD ** (-0.5)
    gathered = (
        lax.all_gather(gain_self, ("dp", "seq"), axis=0, tiled=True),
        lax.all_gather(gain_cross, ("dp", "seq"), axis=0, tiled=True),
        lax.all_gather(gain_mlp, ("dp", "seq"), axis=0, tiled=True),
        lax.all_gather(w_qkv, ("dp", "seq"), axis=0, tiled=True),
        lax.all_gather(w_self_out, ("dp", "seq"), axis=0, tiled=True),
        lax.all_gather(w_cross_q, ("dp", "seq"), axis=0, tiled=True),
        lax.all_gather(w_cross_kv, ("dp", "seq"), axis=0, tiled=True),
        lax.all_gather(w_cross_out, ("dp", "seq"), axis=0, tiled=True),
        lax.all_gather(w_up, ("dp", "seq"), axis=0, tiled=True),
        lax.all_gather(w_down, ("dp", "seq"), axis=0, tiled=True),
    )
    (
        gain_one,
        gain_two,
        gain_three,
        full_qkv,
        full_self_out,
        full_cross_q,
        full_cross_kv,
        full_cross_out,
        full_up,
        full_down,
    ) = gathered
    position = jnp.arange(full_len)
    causal = (position[:, None] >= position[None, :])[None, None]
    split_shape = (count_local, full_len, groups, head_span)
    head_shape = (count_caps, full_len, local_heads, HEAD)
    back_shape = (count_caps, full_len, 1, head_span)
    token_shape = (count_local, full_len, model_width)
    tokens = captions.astype(jnp.float32)
    normed_one = layer_norm(tokens, gain_one.astype(jnp.float32)).astype(jnp.bfloat16)
    packed = linear(normed_one, full_qkv).astype(jnp.bfloat16)
    query_part = packed[..., :model_width].reshape(split_shape)
    key_part = packed[..., model_width : 2 * model_width].reshape(split_shape)
    value_part = packed[..., 2 * model_width :].reshape(split_shape)
    query_recv, key_recv, value_recv = (
        lax.all_to_all(query_part, "seq", split_axis=2, concat_axis=0, tiled=True),
        lax.all_to_all(key_part, "seq", split_axis=2, concat_axis=0, tiled=True),
        lax.all_to_all(value_part, "seq", split_axis=2, concat_axis=0, tiled=True),
    )
    query_heads = query_recv.reshape(head_shape)
    key_heads = key_recv.reshape(head_shape)
    value_heads = value_recv.reshape(head_shape)
    self_result, self_totals = attend_forward(query_heads, key_heads, value_heads, causal, factor)
    self_back = lax.all_to_all(
        self_result.reshape(back_shape), "seq", split_axis=0, concat_axis=2, tiled=True
    )
    self_tokens = self_back.reshape(token_shape)
    after_self = tokens + linear(self_tokens, full_self_out)
    normed_two = layer_norm(after_self, gain_two.astype(jnp.float32)).astype(jnp.bfloat16)
    cross_full = linear(normed_two, full_cross_q).astype(jnp.bfloat16)
    cross_queries = lax.all_to_all(
        cross_full.reshape(split_shape), "seq", split_axis=2, concat_axis=0, tiled=True
    ).reshape(head_shape)
    image_allowed = (tissue_mask > 0)[:, None, None, :]
    local_pairs = pair_columns(full_cross_kv, seq_index, head_span, model_width)
    image_pairs = linear(images, local_pairs).astype(jnp.bfloat16)
    image_shape = (count_caps, patch_count, local_heads, HEAD)
    cross_keys = image_pairs[..., :head_span].reshape(image_shape)
    cross_values = image_pairs[..., head_span:].reshape(image_shape)
    cross_result, cross_totals = attend_forward(
        cross_queries, cross_keys, cross_values, image_allowed, factor
    )
    cross_back = lax.all_to_all(
        cross_result.reshape(back_shape), "seq", split_axis=0, concat_axis=2, tiled=True
    )
    cross_tokens = cross_back.reshape(token_shape)
    after_cross = after_self + linear(cross_tokens, full_cross_out)
    normed_three = layer_norm(after_cross, gain_three.astype(jnp.float32)).astype(jnp.bfloat16)
    hidden = linear(normed_three, full_up)
    active = exact_gelu(hidden).astype(jnp.bfloat16)
    block_out = (after_cross + linear(active, full_down)).astype(jnp.bfloat16)
    backward_set = (
        lax.all_gather(gain_self, ("dp", "seq"), axis=0, tiled=True),
        lax.all_gather(gain_cross, ("dp", "seq"), axis=0, tiled=True),
        lax.all_gather(gain_mlp, ("dp", "seq"), axis=0, tiled=True),
        lax.all_gather(w_qkv, ("dp", "seq"), axis=0, tiled=True),
        lax.all_gather(w_self_out, ("dp", "seq"), axis=0, tiled=True),
        lax.all_gather(w_cross_q, ("dp", "seq"), axis=0, tiled=True),
        lax.all_gather(w_cross_kv, ("dp", "seq"), axis=0, tiled=True),
        lax.all_gather(w_cross_out, ("dp", "seq"), axis=0, tiled=True),
        lax.all_gather(w_up, ("dp", "seq"), axis=0, tiled=True),
        lax.all_gather(w_down, ("dp", "seq"), axis=0, tiled=True),
    )
    (
        gain_one,
        gain_two,
        gain_three,
        full_qkv,
        full_self_out,
        full_cross_q,
        full_cross_kv,
        full_cross_out,
        full_up,
        full_down,
    ) = backward_set
    grad_down = weight_grad(active, cotangent)
    grad_active = linear_back(cotangent, full_down)
    unused, gelu_pull = jax.vjp(exact_gelu, hidden)
    grad_hidden = gelu_pull(grad_active)[0].astype(jnp.bfloat16)
    grad_up = weight_grad(normed_three, grad_hidden)
    grad_normed_three = linear_back(grad_hidden, full_up)
    norm_grad_three, grad_gain_three = norm_back(
        after_cross, gain_three.astype(jnp.float32), grad_normed_three
    )
    grad_after_cross = cotangent.astype(jnp.float32) + norm_grad_three
    cross_branch = grad_after_cross.astype(jnp.bfloat16)
    grad_cross_out = weight_grad(cross_tokens, cross_branch)
    cross_full_grad = linear_back(cross_branch, full_cross_out).astype(jnp.bfloat16)
    cross_upstream = lax.all_to_all(
        cross_full_grad.reshape(split_shape), "seq", split_axis=2, concat_axis=0, tiled=True
    ).reshape(head_shape)
    grad_cross_queries, grad_cross_keys, grad_cross_values = attend_back(
        cross_queries, cross_keys, cross_values, image_allowed, factor, cross_totals, cross_upstream
    )
    pair_grads = jnp.concatenate(
        [
            grad_cross_keys.reshape(count_caps, patch_count, head_span),
            grad_cross_values.reshape(count_caps, patch_count, head_span),
        ],
        axis=-1,
    )
    local_pairs = pair_columns(full_cross_kv, seq_index, head_span, model_width)
    grad_local_pairs = weight_grad(images, pair_grads)
    image_terms = linear_back(pair_grads, local_pairs)
    grad_images = lax.psum_scatter(
        image_terms.astype(jnp.bfloat16), "seq", scatter_dimension=2, tiled=True
    ).astype(jnp.float32)
    grad_cross_kv = jnp.zeros((model_width, 2 * model_width), jnp.float32)
    grad_cross_kv = lax.dynamic_update_slice_in_dim(
        grad_cross_kv, grad_local_pairs[:, :head_span], seq_index * head_span, 1
    )
    grad_cross_kv = lax.dynamic_update_slice_in_dim(
        grad_cross_kv, grad_local_pairs[:, head_span:], model_width + seq_index * head_span, 1
    )
    query_grad_back = lax.all_to_all(
        grad_cross_queries.reshape(back_shape), "seq", split_axis=0, concat_axis=2, tiled=True
    )
    query_grad_tokens = query_grad_back.reshape(token_shape)
    grad_cross_q = weight_grad(normed_two, query_grad_tokens)
    grad_normed_two = linear_back(query_grad_tokens, full_cross_q)
    norm_grad_two, grad_gain_two = norm_back(
        after_self, gain_two.astype(jnp.float32), grad_normed_two
    )
    grad_after_self = grad_after_cross + norm_grad_two
    self_branch = grad_after_self.astype(jnp.bfloat16)
    grad_self_out = weight_grad(self_tokens, self_branch)
    self_full_grad = linear_back(self_branch, full_self_out).astype(jnp.bfloat16)
    self_upstream = lax.all_to_all(
        self_full_grad.reshape(split_shape), "seq", split_axis=2, concat_axis=0, tiled=True
    ).reshape(head_shape)
    grad_queries, grad_keys, grad_values = attend_back(
        query_heads, key_heads, value_heads, causal, factor, self_totals, self_upstream
    )
    query_back, key_back, value_back = (
        lax.all_to_all(
            grad_queries.reshape(back_shape), "seq", split_axis=0, concat_axis=2, tiled=True
        ),
        lax.all_to_all(
            grad_keys.reshape(back_shape), "seq", split_axis=0, concat_axis=2, tiled=True
        ),
        lax.all_to_all(
            grad_values.reshape(back_shape), "seq", split_axis=0, concat_axis=2, tiled=True
        ),
    )
    packed_grad = jnp.concatenate(
        [
            query_back.reshape(token_shape),
            key_back.reshape(token_shape),
            value_back.reshape(token_shape),
        ],
        axis=-1,
    )
    grad_qkv = weight_grad(normed_one, packed_grad)
    grad_normed_one = linear_back(packed_grad, full_qkv)
    norm_grad_one, grad_gain_one = norm_back(tokens, gain_one.astype(jnp.float32), grad_normed_one)
    grad_captions = grad_after_self + norm_grad_one
    shards = (
        lax.psum_scatter(grad_gain_one, ("dp", "seq"), scatter_dimension=0, tiled=True),
        lax.psum_scatter(grad_gain_two, ("dp", "seq"), scatter_dimension=0, tiled=True),
        lax.psum_scatter(grad_gain_three, ("dp", "seq"), scatter_dimension=0, tiled=True),
        lax.psum_scatter(grad_qkv, ("dp", "seq"), scatter_dimension=0, tiled=True),
        lax.psum_scatter(grad_self_out, ("dp", "seq"), scatter_dimension=0, tiled=True),
        lax.psum_scatter(grad_cross_q, ("dp", "seq"), scatter_dimension=0, tiled=True),
        lax.psum_scatter(grad_cross_kv, ("dp", "seq"), scatter_dimension=0, tiled=True),
        lax.psum_scatter(grad_cross_out, ("dp", "seq"), scatter_dimension=0, tiled=True),
        lax.psum_scatter(grad_up, ("dp", "seq"), scatter_dimension=0, tiled=True),
        lax.psum_scatter(grad_down, ("dp", "seq"), scatter_dimension=0, tiled=True),
    )
    return (
        block_out,
        grad_captions,
        grad_images,
        shards[0],
        shards[1],
        shards[2],
        shards[3],
        shards[4],
        shards[5],
        shards[6],
        shards[7],
        shards[8],
        shards[9],
    )


def solution(mesh):
    return jax.shard_map(
        on_device,
        mesh=mesh,
        in_specs=(
            P(("dp", "seq"), None, None),
            P("dp", None, None),
            P("dp", None),
            P(("dp", "seq")),
            P(("dp", "seq")),
            P(("dp", "seq")),
            P(("dp", "seq"), None),
            P(("dp", "seq"), None),
            P(("dp", "seq"), None),
            P(("dp", "seq"), None),
            P(("dp", "seq"), None),
            P(("dp", "seq"), None),
            P(("dp", "seq"), None),
            P(("dp", "seq"), None, None),
        ),
        out_specs=(
            P(("dp", "seq"), None, None),
            P(("dp", "seq"), None, None),
            P("dp", None, "seq"),
            P(("dp", "seq")),
            P(("dp", "seq")),
            P(("dp", "seq")),
            P(("dp", "seq"), None),
            P(("dp", "seq"), None),
            P(("dp", "seq"), None),
            P(("dp", "seq"), None),
            P(("dp", "seq"), None),
            P(("dp", "seq"), None),
            P(("dp", "seq"), None),
        ),
        check_vma=False,
    )
```

profile of v0, /device:TPU:0, one launch (start us, length us, event | category | flops | bytes accessed | tf_op | source)
XLA Modules:
  0.0 1383.9 jit_solution(16979897317913632275)
XLA Ops:
  13.7 42.1 %all-reduce.7 = (bf16[768]{0:T(1024)(128)(2,1)S(1)}, bf16[768]{0:T(1024)(128)(2,1)}, bf16[768]{0:T(1024)(128)(2,1)}) all-reduce(bf16[768]{0:T(1024)(128)(2,1)S(1)} %dynamic-update-slice, bf16[768]{0:T(1024)(128)(2,1)S(1)} %dynamic-update-slice.1, bf16[768]{0:T(1024)(128)(2,1)S(1)} %dynamic-update-slice.2), channel_id=1, replica_groups=mesh['dp'=8,'seq'=4] {'dp','seq'}, use_global_device_ids=true, to_apply=%add | all-reduce | flops 2304 | bytes 9216
  58.6 15.4 %all-gather.8.cloned.1.call-done = bf16[768,2304]{1,0:T(8,128)(2,1)} async-done(((bf16[24,2304]{1,0:T(8,128)(2,1)}), bf16[768,2304]{1,0:T(8,128)(2,1)}) %all-gather.8.cloned.1.call-update) | async-done | bytes 3538960 | tf_op jit(solution)/shard_map/all_gather | solution.py:122
  83.8 8.9 all-to-all-done.2
  137.1 52.2 %all-gather.10.cloned.1.call-done = bf16[768,768]{1,0:T(8,128)(2,1)} async-done(((bf16[24,768]{1,0:T(8,128)(2,1)}), bf16[768,768]{1,0:T(8,128)(2,1)}) %all-gather.10.cloned.1.call-update) | async-done | bytes 1179664 | tf_op jit(solution)/shard_map/all_gather | solution.py:123
  191.6 53.5 %all-gather.14.cloned.1.call-done = bf16[768,768]{1,0:T(8,128)(2,1)} async-done(((bf16[24,768]{1,0:T(8,128)(2,1)}), bf16[768,768]{1,0:T(8,128)(2,1)}) %all-gather.14.cloned.1.call-update) | async-done | bytes 1179664 | tf_op jit(solution)/shard_map/all_gather | solution.py:124
  273.1 9.5 all-to-all-done.5
  282.6 18.4 %all-gather.16.cloned.1.call-done = bf16[768,768]{1,0:T(8,128)(2,1)} async-done(((bf16[24,768]{1,0:T(8,128)(2,1)}), bf16[768,768]{1,0:T(8,128)(2,1)}) %all-gather.16.cloned.1.call-update) | async-done | bytes 1179664 | tf_op jit(solution)/shard_map/all_gather | solution.py:126
  305.0 61.3 %all-gather.18.cloned.1.call-done = bf16[768,3072]{1,0:T(8,128)(2,1)} async-done(((bf16[24,3072]{1,0:T(8,128)(2,1)}), bf16[768,3072]{1,0:T(8,128)(2,1)}) %all-gather.18.cloned.1.call-update) | async-done | bytes 4718608 | tf_op jit(solution)/shard_map/all_gather | solution.py:127
  374.2 11.6 multiply_convert_fusion
  385.8 45.8 %all-gather.20.cloned.1.call-done = bf16[3072,768]{1,0:T(8,128)(2,1)} async-done(((bf16[96,768]{1,0:T(8,128)(2,1)}), bf16[3072,768]{1,0:T(8,128)(2,1)}) %all-gather.20.cloned.1.call-update) | async-done | bytes 4718608 | tf_op jit(solution)/shard_map/all_gather | solution.py:128
  431.6 8.2 add_convert_fusion
  455.8 8.5 all-to-all-done.6
  471.0 8.2 fusion.57
  493.6 9.2 fusion.69
  502.8 17.0 %all_to_all.180 = bf16[12,128,1,192]{1,3,2,0:T(8,128)(2,1)S(1)} all-to-all(bf16[12,128,1,192]{1,3,2,0:T(8,128)(2,1)S(1)} %bitcast.236), channel_id=1, replica_groups=mesh['dp'=8,'seq'=4] {'seq'}, dimensions={0} | all-to-all | bytes 1179648 | tf_op jit(solution)/shard_map/all_to_all | solution.py:254
  556.2 8.1 all-to-all-done.8
  592.3 9.7 all-to-all-done.10
  646.1 41.3 %all-reduce.6 = (f32[768]{0:T(1024)S(1)}, f32[768]{0:T(1024)S(1)}, f32[768]{0:T(1024)S(1)}) all-reduce(f32[768]{0:T(1024)S(1)} %get-tuple-element.19, f32[768]{0:T(1024)} %get-tuple-element.15, f32[768]{0:T(1024)} %get-tuple-element.17), channel_id=3, replica_groups=mesh['dp'=8,'seq'=4] {'dp','seq'}, use_global_device_ids=true, to_apply=%region_20.21.clone | all-reduce | flops 2304 | bytes 18432
  693.6 58.0 %reduce-scatter.15.cloned.1.call-done = f32[24,768]{1,0:T(8,128)} async-done(((f32[768,768]{1,0:T(8,128)}), f32[24,768]{1,0:T(8,128)}) %reduce-scatter.15.cloned.1.call-update) | async-done | bytes 73744 | tf_op jit(solution)/shard_map/reduce_scatter | solution.py:302
  751.6 104.8 %reduce-scatter.13.cloned.1.call-done = f32[24,768]{1,0:T(8,128)} async-done(((f32[768,768]{1,0:T(8,128)}), f32[24,768]{1,0:T(8,128)}) %reduce-scatter.13.cloned.1.call-update) | async-done | bytes 73744 | tf_op jit(solution)/shard_map/reduce_scatter | solution.py:301
  856.4 111.9 %reduce-scatter.17.cloned.1.call-done = f32[24,1536]{1,0:T(8,128)} async-done(((f32[768,1536]{1,0:T(8,128)}), f32[24,1536]{1,0:T(8,128)}) %reduce-scatter.17.cloned.1.call-update) | async-done | bytes 147472 | tf_op jit(solution)/shard_map/reduce_scatter | solution.py:303
  968.3 125.6 %reduce-scatter.11.cloned.1.call-done = f32[24,2304]{1,0:T(8,128)} async-done(((f32[768,2304]{1,0:T(8,128)}), f32[24,2304]{1,0:T(8,128)}) %reduce-scatter.11.cloned.1.call-update) | async-done | bytes 221200 | tf_op jit(solution)/shard_map/reduce_scatter | solution.py:300
  1093.9 141.2 %reduce-scatter.21.cloned.1.call-done = f32[24,3072]{1,0:T(8,128)} async-done(((f32[768,3072]{1,0:T(8,128)}), f32[24,3072]{1,0:T(8,128)}) %reduce-scatter.21.cloned.1.call-update) | async-done | bytes 294928 | tf_op jit(solution)/shard_map/reduce_scatter | solution.py:305
  1235.1 141.9 %reduce-scatter.23.cloned.1.call-done = f32[96,768]{1,0:T(8,128)} async-done(((f32[3072,768]{1,0:T(8,128)}), f32[96,768]{1,0:T(8,128)}) %reduce-scatter.23.cloned.1.call-update) | async-done | bytes 294928 | tf_op jit(solution)/shard_map/reduce_scatter | solution.py:306
  (281 shorter events, 256.4 us)
Async XLA Ops:
  7.2 66.8 %all-gather.8.cloned.1.call-start = ((), (), s32[]{:S(2)}) async-start(), calls=%async_computation.20 | async-start | bytes 3649536 | tf_op jit(solution)/shard_map/all_gather | solution.py:122
  7.9 125.4 %all-gather.12.cloned.1.call-start = ((), (), s32[]{:S(2)}) async-start(), calls=%async_computation.22 | async-start | bytes 2433024 | tf_op jit(solution)/shard_map/all_gather | solution.py:125
  8.7 180.6 %all-gather.10.cloned.1.call-start = ((), (), s32[]{:S(2)}) async-start(), calls=%async_computation.21 | async-start | bytes 1216512 | tf_op jit(solution)/shard_map/all_gather | solution.py:123
  9.4 235.7 %all-gather.14.cloned.1.call-start = ((), (), s32[]{:S(2)}) async-start(), calls=%async_computation.23 | async-start | bytes 1216512 | tf_op jit(solution)/shard_map/all_gather | solution.py:124
  10.0 291.0 %all-gather.16.cloned.1.call-start = ((), (), s32[]{:S(2)}) async-start(), calls=%async_computation.24 | async-start | bytes 1216512 | tf_op jit(solution)/shard_map/all_gather | solution.py:126
  10.6 355.7 %all-gather.18.cloned.1.call-start = ((), (), s32[]{:S(2)}) async-start(), calls=%async_computation.25 | async-start | bytes 4866048 | tf_op jit(solution)/shard_map/all_gather | solution.py:127
  79.2 13.5 all-to-all-start.2
  92.7 14.1 %all-to-all-start.1 = ((bf16[3,128,4,192]{1,3,0,2:T(8,128)(2,1)}), bf16[3,128,4,192]{1,3,0,2:T(8,128)(2,1)S(1)}, u32[]{:S(2)}, u32[]{:S(2)}) async-start(bf16[3,128,4,192]{1,3,0,2:T(8,128)(2,1)} %copy.138), calls=%async_computation.1 | async-start | bytes 1179648 | tf_op jit(solution)/shard_map/all_to_all | solution.py:155
  96.2 335.4 %all-gather.20.cloned.1.call-start = ((), (), s32[]{:S(2)}) async-start(), calls=%async_computation.26 | async-start | bytes 4866048 | tf_op jit(solution)/shard_map/all_gather | solution.py:128
  106.8 14.7 %all-to-all-start = ((bf16[3,128,4,192]{1,3,0,2:T(8,128)(2,1)}), bf16[3,128,4,192]{1,3,0,2:T(8,128)(2,1)}, u32[]{:S(2)}, u32[]{:S(2)}) async-start(bf16[3,128,4,192]{1,3,0,2:T(8,128)(2,1)} %copy.136), calls=%async_computation | async-start | bytes 1179648 | tf_op jit(solution)/shard_map/all_to_all | solution.py:157
  123.9 13.1 all-to-all-start.3
  248.2 14.2 %all-to-all-start.4 = ((bf16[3,128,4,192]{1,3,0,2:T(8,128)(2,1)}), bf16[3,128,4,192]{1,3,0,2:T(8,128)(2,1)}, u32[]{:S(2)}, u32[]{:S(2)}) async-start(bf16[3,128,4,192]{1,3,0,2:T(8,128)(2,1)} %copy.147), calls=%async_computation.4 | async-start | bytes 1179648 | tf_op jit(solution)/shard_map/all_to_all | solution.py:170
  269.2 13.4 all-to-all-start.5
  454.7 235.9 %reduce-scatter.9.cloned.1.call-start = ((), (), s32[]{:S(2)}) async-start(), calls=%async_computation.27 | async-start | bytes 5898240 | tf_op jit(solution)/shard_map/reduce_scatter | solution.py:244
  490.1 203.5 %reduce-scatter.19.cloned.1.call-start = ((), (), s32[]{:S(2)}) async-start(), calls=%async_computation.32 | async-start | bytes 2433024 | tf_op jit(solution)/shard_map/reduce_scatter | solution.py:304
  493.5 258.1 %reduce-scatter.15.cloned.1.call-start = ((), (), s32[]{:S(2)}) async-start(), calls=%async_computation.30 | async-start | bytes 2433024 | tf_op jit(solution)/shard_map/reduce_scatter | solution.py:302
  522.3 334.1 %reduce-scatter.13.cloned.1.call-start = ((), (), s32[]{:S(2)}) async-start(), calls=%async_computation.29 | async-start | bytes 2433024 | tf_op jit(solution)/shard_map/reduce_scatter | solution.py:301
  529.3 439.0 %reduce-scatter.17.cloned.1.call-start = ((), (), s32[]{:S(2)}) async-start(), calls=%async_computation.31 | async-start | bytes 4866048 | tf_op jit(solution)/shard_map/reduce_scatter | solution.py:303
  551.2 13.1 all-to-all-start.8
  571.9 13.8 all-to-all-start.9
  585.7 16.3 %all-to-all-start.10 = ((bf16[12,128,1,192]{1,3,2,0:T(8,128)(2,1)}), bf16[12,128,1,192]{1,3,2,0:T(8,128)(2,1)}, u32[]{:S(2)}, u32[]{:S(2)}) async-start(bf16[12,128,1,192]{1,3,2,0:T(8,128)(2,1)} %bitcast.234), calls=%async_computation.10 | async-start | bytes 1179648 | tf_op jit(solution)/shard_map/all_to_all | solution.py:277
  605.5 488.3 %reduce-scatter.11.cloned.1.call-start = ((), (), s32[]{:S(2)}) async-start(), calls=%async_computation.28 | async-start | bytes 7299072 | tf_op jit(solution)/shard_map/reduce_scatter | solution.py:300
  620.5 614.6 %reduce-scatter.21.cloned.1.call-start = ((), (), s32[]{:S(2)}) async-start(), calls=%async_computation.33 | async-start | bytes 9732096 | tf_op jit(solution)/shard_map/reduce_scatter | solution.py:305
  628.7 748.3 %reduce-scatter.23.cloned.1.call-start = ((), (), s32[]{:S(2)}) async-start(), calls=%async_computation.34 | async-start | bytes 9732096 | tf_op jit(solution)/shard_map/reduce_scatter | solution.py:306
  (65 other events, 1058.6 us)
Sparse Core Ops, SparseCore 0:
  10.9 63.0 all-gather.7
  76.9 56.3 all-gather.11
  136.2 52.9 all-gather.9
  192.0 53.0 all-gather.13
  247.8 53.0 all-gather.15
  303.7 62.5 all-gather.17
  369.2 62.3 all-gather.19
  490.2 51.1 reduce-scatter.8
  548.2 99.5 reduce-scatter.18
  653.5 98.0 reduce-scatter.14
  758.3 98.0 reduce-scatter.12
  862.3 105.9 reduce-scatter.16
  975.5 118.3 reduce-scatter.10
  1100.2 134.8 reduce-scatter.20
  1242.4 134.4 reduce-scatter.22
where the time goes:
time: 1390 us; the launch traced here: 1380 us
  waiting for transfers between devices  1010 us (73%)
  matrix products  132 us (9%)
  blocking collectives  100 us (7%)
  local copies, waits for them, and re-layouts  52.1 us (4%)
  starting transfers between devices  43.1 us (3%)
  other arithmetic  26.8 us (2%)
  between operations  15.3 us (1%)
    reduce_scatter x1, waiting for transfers between devices, on_device(): lax.psum_scatter(grad_down, ('dp', 'seq'), scatter_dimension=0, tiled=True)  142 us
    reduce_scatter x1, waiting for transfers between devices, on_device(): lax.psum_scatter(grad_up, ('dp', 'seq'), scatter_dimension=0, tiled=True)  141 us
    reduce_scatter x1, waiting for transfers between devices, on_device(): lax.psum_scatter(grad_qkv, ('dp', 'seq'), scatter_dimension=0, tiled=True)  126 us
    reduce_scatter x1, waiting for transfers between devices, on_device(): lax.psum_scatter(grad_cross_kv, ('dp', 'seq'), scatter_dimension=0, tiled...  112 us
    reduce_scatter x1, waiting for transfers between devices, on_device(): lax.psum_scatter(grad_self_out, ('dp', 'seq'), scatter_dimension=0, tiled...  105 us
    unnamed x2, blocking collectives  83.5 us
    all_gather x1, waiting for transfers between devices, on_device(): lax.all_gather(w_up, ('dp', 'seq'), axis=0, tiled=True)  61.3 us
    reduce_scatter x1, waiting for transfers between devices, on_device(): lax.psum_scatter(grad_cross_q, ('dp', 'seq'), scatter_dimension=0, tiled=...  58 us
  transfers between devices with their start and end apart: 26, of which 24 were waited for; matrix products, arithmetic and copies ran while one was open for 11% of the time, Pallas kernels for 0%

commit v1 on v0

v1 whole, which is shorter than its diff:
```python
import jax
import jax.numpy as jnp
from jax import lax
from jax.sharding import PartitionSpec as P

HEADS = 12
HEAD = 64
EPS = 1e-05
BOTH = ("dp", "seq")
f32 = jnp.float32
bf16 = jnp.bfloat16


def norm_stats(v):
    mean = jnp.mean(v, axis=-1, keepdims=True)
    centered = v - mean
    r = lax.rsqrt(jnp.mean(centered * centered, axis=-1, keepdims=True) + EPS)
    return centered * r, r


def norm_back(xhat, r, gain, e):
    u = e * gain
    mu = jnp.mean(u, axis=-1, keepdims=True)
    mx = jnp.mean(u * xhat, axis=-1, keepdims=True)
    return r * (u - mu - xhat * mx), jnp.sum(e * xhat, axis=(0, 1))


def mm(a, b):
    return jnp.einsum("btd,de->bte", a, b, preferred_element_type=f32)


def mm_t(a, b):
    return jnp.einsum("bte,de->btd", a, b, preferred_element_type=f32)


def wgrad(a, b):
    return jnp.einsum("btd,bte->de", a, b, preferred_element_type=f32)


def split_heads(a):
    b, t, _ = a.shape
    return a.reshape(b, t, -1, HEAD)


def attend(q, k, v, allowed):
    s = jnp.einsum("bqhe,bkhe->bhqk", q, k, preferred_element_type=f32) * HEAD ** (-0.5)
    s = jnp.where(allowed, s, -1e30)
    ex = jnp.exp(s - jnp.max(s, axis=-1, keepdims=True))
    p = ex / jnp.sum(ex, axis=-1, keepdims=True)
    o = jnp.einsum("bhqk,bkhe->bqhe", p.astype(bf16), v, preferred_element_type=f32)
    return p, o.astype(bf16)


def attend_back(q, k, v, p, g):
    dp = jnp.einsum("bqhe,bkhe->bhqk", g, v, preferred_element_type=f32)
    ds = (p * (dp - jnp.sum(dp * p, axis=-1, keepdims=True)) * HEAD ** (-0.5)).astype(bf16)
    dq = jnp.einsum("bhqk,bkhe->bqhe", ds, k, preferred_element_type=f32).astype(bf16)
    dk = jnp.einsum("bhqk,bqhe->bkhe", ds, q, preferred_element_type=f32).astype(bf16)
    dv = jnp.einsum("bhqk,bqhe->bkhe", p.astype(bf16), g, preferred_element_type=f32).astype(bf16)
    return dq, dk, dv


def layer(x0, img, mask, gains, weights, cot):
    g1, g2, g3 = (g.astype(f32) for g in gains)
    w_qkv, w_so, w_cq, w_ckv, w_co, w_up, w_down = weights
    b, t, d = x0.shape
    x = x0.astype(f32)
    pos = jnp.arange(t)
    causal = (pos[:, None] >= pos[None, :])[None, None]
    allowed = (mask > 0)[:, None, None, :]
    h1, r1 = norm_stats(x)
    n1 = (h1 * g1).astype(bf16)
    qkv = mm(n1, w_qkv).astype(bf16)
    q1, k1, v1 = (split_heads(qkv[..., i * d : (i + 1) * d]) for i in range(3))
    p1, o1 = attend(q1, k1, v1, causal)
    o1 = o1.reshape(b, t, d)
    x1 = x + mm(o1, w_so)
    h2, r2 = norm_stats(x1)
    n2 = (h2 * g2).astype(bf16)
    q2 = split_heads(mm(n2, w_cq).astype(bf16))
    kv = mm(img, w_ckv).astype(bf16)
    k2, v2 = split_heads(kv[..., :d]), split_heads(kv[..., d:])
    p2, o2 = attend(q2, k2, v2, allowed)
    o2 = o2.reshape(b, t, d)
    x2 = x1 + mm(o2, w_co)
    h3, r3 = norm_stats(x2)
    n3 = (h3 * g3).astype(bf16)
    hpre = mm(n3, w_up)
    cdf = 0.5 * (1.0 + lax.erf(hpre * (0.5**0.5)))
    act = (hpre * cdf).astype(bf16)
    out = (x2 + mm(act, w_down)).astype(bf16)

    gw_down = wgrad(act, cot)
    pdf = jnp.exp(-0.5 * hpre * hpre) * (0.5 / jnp.pi) ** 0.5
    gh = (mm_t(cot, w_down) * (cdf + hpre * pdf)).astype(bf16)
    gw_up = wgrad(n3, gh)
    dx2, gg3 = norm_back(h3, r3, g3, mm_t(gh, w_up))
    gx2 = cot.astype(f32) + dx2
    gx2b = gx2.astype(bf16)
    gw_co = wgrad(o2, gx2b)
    go2 = split_heads(mm_t(gx2b, w_co).astype(bf16))
    dq2, dk2, dv2 = attend_back(q2, k2, v2, p2, go2)
    dq2 = dq2.reshape(b, t, d)
    dkv = jnp.concatenate([dk2.reshape(b, -1, d), dv2.reshape(b, -1, d)], axis=-1)
    gw_ckv = wgrad(img, dkv)
    gimg = mm_t(dkv, w_ckv).astype(bf16)
    gw_cq = wgrad(n2, dq2)
    dx1, gg2 = norm_back(h2, r2, g2, mm_t(dq2, w_cq))
    gx1 = gx2 + dx1
    gx1b = gx1.astype(bf16)
    gw_so = wgrad(o1, gx1b)
    go1 = split_heads(mm_t(gx1b, w_so).astype(bf16))
    dq1, dk1, dv1 = attend_back(q1, k1, v1, p1, go1)
    dqkv = jnp.concatenate([a.reshape(b, t, d) for a in (dq1, dk1, dv1)], axis=-1)
    gw_qkv = wgrad(n1, dqkv)
    dx0, gg1 = norm_back(h1, r1, g1, mm_t(dqkv, w_qkv))
    gx0 = gx1 + dx0
    return out, gx0, gimg, (gg1, gg2, gg3), (gw_qkv, gw_so, gw_cq, gw_ckv, gw_co, gw_up, gw_down)


def on_device(captions, images, tissue_mask, gain_self, gain_cross, gain_mlp, *rest):
    weights, cotangent = rest[:-1], rest[-1]
    count = captions.shape[0]
    start = lax.axis_index("seq") * count
    img = lax.dynamic_slice_in_dim(images, start, count, 0)
    mask = lax.dynamic_slice_in_dim(tissue_mask, start, count, 0)
    gains = jnp.stack([gain_self, gain_cross, gain_mlp], axis=1)
    gains = lax.all_gather(gains, BOTH, axis=0, tiled=True)
    gains = tuple(gains[:, i] for i in range(3))
    full = [lax.all_gather(w, BOTH, axis=0, tiled=True) for w in weights]
    out, gx0, gimg, gg, gw = layer(captions, img, mask, gains, full, cotangent)
    gimg = lax.all_to_all(gimg, "seq", split_axis=2, concat_axis=0, tiled=True).astype(f32)
    gg = lax.psum_scatter(jnp.stack(gg, axis=1), BOTH, scatter_dimension=0, tiled=True)
    shards = [
        lax.psum_scatter(g.astype(bf16), BOTH, scatter_dimension=0, tiled=True).astype(f32)
        for g in gw
    ]
    return (out, gx0, gimg, gg[:, 0], gg[:, 1], gg[:, 2], *shards)


def solution(mesh):
    tok = P(BOTH, None, None)
    vec = P(BOTH)
    mat = P(BOTH, None)
    return jax.shard_map(
        on_device,
        mesh=mesh,
        in_specs=(tok, P("dp", None, None), P("dp", None), vec, vec, vec, *([mat] * 7), tok),
        out_specs=(tok, tok, P("dp", None, "seq"), vec, vec, vec, *([mat] * 7)),
        check_vma=False,
    )
```

time: 1390 us -> 1190 us (0.86)
  waiting for transfers between devices: 1010 us -> 890 us
  starting transfers between devices: 43.1 us -> 5.22 us
  local copies, waits for them, and re-layouts: 52.1 us -> 31.1 us
    reduce_scatter x8 -> x7, waiting for transfers between devices: 683 us -> 558 us  [on_device(): lax.psum_scatter(g.astype(bf16), BOTH, scatter_dimension=0, tiled=True)]
    all_gather x7, waiting for transfers between devices: 252 us -> 327 us  [on_device(): full = [lax.all_gather(w, BOTH, axis=0, tiled=True) for w in weights]]
    all_to_all x11 -> x1, waiting for transfers between devices: 73.9 us -> 0.01 us  [on_device(): lax.all_to_all(gimg, 'seq', split_axis=2, concat_axis=0, tiled=True)]
    all_gather x0 -> x1, blocking collectives: none -> 43.3 us  [on_device(): gains = lax.all_gather(gains, BOTH, axis=0, tiled=True)]
    all_to_all x11 -> x1, starting transfers between devices: 41.8 us -> 4.49 us  [on_device(): lax.all_to_all(gimg, 'seq', split_axis=2, concat_axis=0, tiled=True)]
    unnamed x2 -> x1, blocking collectives: 83.5 us -> 47.4 us
    all_to_all x1 -> x0, blocking collectives: 17 us -> none  [on_device(): lax.all_to_all(grad_cross_queries.reshape(back_shape), 'seq', split_axis=...]
    dot_general x33 -> x31, matrix products: 132 us -> 120 us  [the longest x7 27.3 us: wgrad(): return jnp.einsum('btd,bte->de', a, b, preferred_element_type=f32)]
  transfers between devices with their start and end apart: 26 -> 15, of which waited for: 24 -> 13; matrix products, arithmetic and copies ran while one was open for 11% -> 14% of each run, Pallas kernels for 0% -> 0%
where the time goes in v1:
time: 1190 us; the launch traced here: 1180 us
  waiting for transfers between devices  890 us (75%)
  matrix products  129 us (11%)
  blocking collectives  90.6 us (8%)
  local copies, waits for them, and re-layouts  31.1 us (3%)
  other arithmetic  22.9 us (2%)
  between operations  14.7 us (1%)
    reduce_scatter x7, waiting for transfers between devices, on_device(): lax.psum_scatter(g.astype(bf16), BOTH, scatter_dimension=0, tiled=True)  558 us
    all_gather x7, waiting for transfers between devices, on_device(): full = [lax.all_gather(w, BOTH, axis=0, tiled=True) for w in weights]  327 us
    unnamed x1, blocking collectives  47.4 us
    all_gather x1, blocking collectives, on_device(): gains = lax.all_gather(gains, BOTH, axis=0, tiled=True)  43.3 us
    dot_general x7, matrix products, wgrad(): return jnp.einsum('btd,bte->de', a, b, preferred_element_type=f32)  27.3 us
    dot_general x7, matrix products, mm(): return jnp.einsum('btd,de->bte', a, b, preferred_element_type=f32)  26.1 us
    dot_general x7, matrix products, mm_t(): return jnp.einsum('bte,de->btd', a, b, preferred_element_type=f32)  25.4 us
  transfers between devices with their start and end apart: 15, of which 13 were waited for; matrix products, arithmetic and copies ran while one was open for 14% of the time, Pallas kernels for 0%

profile of v1, /device:TPU:0, one launch (start us, length us, event | category | flops | bytes accessed | tf_op | source)
XLA Modules:
  0.0 1183.5 jit_solution(1222139974295723883)
XLA Ops:
  12.6 43.3 %all-gather = bf16[32,24,3]{1,2,0:T(4,128)(2,1)S(1)} all-gather(bf16[1,24,3]{1,2,0:T(4,128)(2,1)S(1)} %maximum_bitcast_fusion), channel_id=1, replica_groups=mesh['dp'=8,'seq'=4] {'dp','seq'}, dimensions={0}, use_global_device_ids=true | all-gather | bytes 4752 | tf_op jit(solution)/shard_map/all_gather | solution.py:128
  61.2 9.8 all-gather.13.cloned.1.call-done
  76.9 56.0 %all-gather.9.cloned.1.call-done = bf16[768,2304]{1,0:T(8,128)(2,1)} async-done(((bf16[24,2304]{1,0:T(8,128)(2,1)}), bf16[768,2304]{1,0:T(8,128)(2,1)}) %all-gather.9.cloned.1.call-update) | async-done | bytes 3538960 | tf_op jit(solution)/shard_map/all_gather | solution.py:130
  144.9 43.8 %all-gather.11.cloned.1.call-done = bf16[768,768]{1,0:T(8,128)(2,1)} async-done(((bf16[24,768]{1,0:T(8,128)(2,1)}), bf16[768,768]{1,0:T(8,128)(2,1)}) %all-gather.11.cloned.1.call-update) | async-done | bytes 1179664 | tf_op jit(solution)/shard_map/all_gather | solution.py:130
  191.1 53.5 %all-gather.15.cloned.1.call-done = bf16[768,768]{1,0:T(8,128)(2,1)} async-done(((bf16[24,768]{1,0:T(8,128)(2,1)}), bf16[768,768]{1,0:T(8,128)(2,1)}) %all-gather.15.cloned.1.call-update) | async-done | bytes 1179664 | tf_op jit(solution)/shard_map/all_gather | solution.py:130
  257.7 42.7 %all-gather.17.cloned.1.call-done = bf16[768,768]{1,0:T(8,128)(2,1)} async-done(((bf16[24,768]{1,0:T(8,128)(2,1)}), bf16[768,768]{1,0:T(8,128)(2,1)}) %all-gather.17.cloned.1.call-update) | async-done | bytes 1179664 | tf_op jit(solution)/shard_map/all_gather | solution.py:130
  302.7 63.0 %all-gather.19.cloned.1.call-done = bf16[768,3072]{1,0:T(8,128)(2,1)} async-done(((bf16[24,3072]{1,0:T(8,128)(2,1)}), bf16[768,3072]{1,0:T(8,128)(2,1)}) %all-gather.19.cloned.1.call-update) | async-done | bytes 4718608 | tf_op jit(solution)/shard_map/all_gather | solution.py:130
  365.7 6.8 multiply_convert_fusion
  372.5 58.5 %all-gather.21.cloned.1.call-done = bf16[3072,768]{1,0:T(8,128)(2,1)} async-done(((bf16[96,768]{1,0:T(8,128)(2,1)}), bf16[3072,768]{1,0:T(8,128)(2,1)}) %all-gather.21.cloned.1.call-update) | async-done | bytes 4718608 | tf_op jit(solution)/shard_map/all_gather | solution.py:130
  431.0 7.0 fusion.9
  451.7 7.1 fusion.69
  472.0 6.7 fusion.51
  497.2 5.7 fusion.72
  510.3 6.2 bitcast_convert_fusion.1
  517.6 6.6 bitcast_convert_fusion
  537.8 5.7 fusion.83
  543.5 47.4 %all-reduce = f32[768,3]{0,1:T(4,128)S(1)} all-reduce(f32[768,3]{0,1:T(4,128)S(1)} %pad_maximum_fusion.6), channel_id=2, replica_groups=mesh['dp'=8,'seq'=4] {'dp','seq'}, use_global_device_ids=true, to_apply=%region_21.22.clone | all-reduce | flops 2304 | bytes 18432
  595.7 5.2 fusion.66
  609.2 30.3 %reduce-scatter.13.cloned.1.call-done = bf16[24,768]{1,0:T(8,128)(2,1)} async-done(((bf16[768,768]{1,0:T(8,128)(2,1)}), bf16[24,768]{1,0:T(8,128)(2,1)}) %reduce-scatter.13.cloned.1.call-update) | async-done | bytes 36880 | tf_op jit(solution)/shard_map/reduce_scatter | solution.py:135
  640.9 98.8 %reduce-scatter.11.cloned.1.call-done = bf16[24,768]{1,0:T(8,128)(2,1)} async-done(((bf16[768,768]{1,0:T(8,128)(2,1)}), bf16[24,768]{1,0:T(8,128)(2,1)}) %reduce-scatter.11.cloned.1.call-update) | async-done | bytes 36880 | tf_op jit(solution)/shard_map/reduce_scatter | solution.py:135
  741.1 101.9 %reduce-scatter.15.cloned.1.call-done = bf16[24,1536]{1,0:T(8,128)(2,1)} async-done(((bf16[768,1536]{1,0:T(8,128)(2,1)}), bf16[24,1536]{1,0:T(8,128)(2,1)}) %reduce-scatter.15.cloned.1.call-update) | async-done | bytes 73744 | tf_op jit(solution)/shard_map/reduce_scatter | solution.py:135
  844.6 106.8 %reduce-scatter.9.cloned.1.call-done = bf16[24,2304]{1,0:T(8,128)(2,1)} async-done(((bf16[768,2304]{1,0:T(8,128)(2,1)}), bf16[24,2304]{1,0:T(8,128)(2,1)}) %reduce-scatter.9.cloned.1.call-update) | async-done | bytes 110608 | tf_op jit(solution)/shard_map/reduce_scatter | solution.py:135
  953.0 110.7 %reduce-scatter.19.cloned.1.call-done = bf16[24,3072]{1,0:T(8,128)(2,1)} async-done(((bf16[768,3072]{1,0:T(8,128)(2,1)}), bf16[24,3072]{1,0:T(8,128)(2,1)}) %reduce-scatter.19.cloned.1.call-update) | async-done | bytes 147472 | tf_op jit(solution)/shard_map/reduce_scatter | solution.py:135
  1065.3 109.8 %reduce-scatter.21.cloned.1.call-done = bf16[96,768]{1,0:T(8,128)(2,1)} async-done(((bf16[3072,768]{1,0:T(8,128)(2,1)}), bf16[96,768]{1,0:T(8,128)(2,1)}) %reduce-scatter.21.cloned.1.call-update) | async-done | bytes 147472 | tf_op jit(solution)/shard_map/reduce_scatter | solution.py:135
  (207 shorter events, 135.5 us)
Async XLA Ops:
  7.2 63.8 %all-gather.13.cloned.1.call-start = ((), (), s32[]{:S(2)}) async-start(), calls=%async_computation.10 | async-start | bytes 2433024 | tf_op jit(solution)/shard_map/all_gather | solution.py:130
  7.9 125.0 %all-gather.9.cloned.1.call-start = ((), (), s32[]{:S(2)}) async-start(), calls=%async_computation.8 | async-start | bytes 3649536 | tf_op jit(solution)/shard_map/all_gather | solution.py:130
  8.7 180.1 %all-gather.11.cloned.1.call-start = ((), (), s32[]{:S(2)}) async-start(), calls=%async_computation.9 | async-start | bytes 1216512 | tf_op jit(solution)/shard_map/all_gather | solution.py:130
  9.4 235.2 %all-gather.15.cloned.1.call-start = ((), (), s32[]{:S(2)}) async-start(), calls=%async_computation.11 | async-start | bytes 1216512 | tf_op jit(solution)/shard_map/all_gather | solution.py:130
  10.0 290.4 %all-gather.17.cloned.1.call-start = ((), (), s32[]{:S(2)}) async-start(), calls=%async_computation.12 | async-start | bytes 1216512 | tf_op jit(solution)/shard_map/all_gather | solution.py:130
  10.6 355.1 %all-gather.19.cloned.1.call-start = ((), (), s32[]{:S(2)}) async-start(), calls=%async_computation.13 | async-start | bytes 4866048 | tf_op jit(solution)/shard_map/all_gather | solution.py:130
  11.1 419.9 %all-gather.21.cloned.1.call-start = ((), (), s32[]{:S(2)}) async-start(), calls=%async_computation.14 | async-start | bytes 4866048 | tf_op jit(solution)/shard_map/all_gather | solution.py:130
  11.9 595.9 %reduce-scatter.17.cloned.1.call-start = ((), (), s32[]{:S(2)}) async-start(), calls=%async_computation.19 | async-start | bytes 1216512 | tf_op jit(solution)/shard_map/reduce_scatter | solution.py:135
  58.5 74.4 %copy-start.31 = (f32[768]{0:T(1024)}, f32[768]{0:T(1024)S(1)}, u32[]{:S(2)}) copy-start(f32[768]{0:T(1024)S(1)} %get-tuple-element.24) | copy-start | bytes 9220
  61.2 71.8 %copy-start.36 = (f32[3,128]{1,0:T(4,128)}, f32[3,128]{1,0:T(4,128)S(1)}, u32[]{:S(2)}) copy-start(f32[3,128]{1,0:T(4,128)S(1)} %add_rsqrt_fusion.2) | copy-start | bytes 4612
  74.6 58.3 %copy-start.2 = (bf16[3,128,768]{2,1,0:T(8,128)(2,1)S(1)}, bf16[3,128,768]{2,1,0:T(8,128)(2,1)}, u32[]{:S(2)}) copy-start(bf16[3,128,768]{2,1,0:T(8,128)(2,1)} %param.14) | copy-start | bytes 1769476
  76.9 177.9 %copy-start.6 = (bf16[3,196,768]{1,2,0:T(8,128)(2,1)}, bf16[3,196,768]{1,2,0:T(8,128)(2,1)S(1)}, u32[]{:S(2)}) copy-start(bf16[3,196,768]{1,2,0:T(8,128)(2,1)S(1)} %copy.149) | copy-start | bytes 2709508
  191.1 58.6 %copy-start.28 = (f32[3,128]{1,0:T(4,128)}, f32[3,128]{1,0:T(4,128)S(1)}, u32[]{:S(2)}) copy-start(f32[3,128]{1,0:T(4,128)S(1)} %add_rsqrt_fusion.1) | copy-start | bytes 4612
  300.4 65.3 %copy-start.33 = (f32[768]{0:T(1024)S(1)}, f32[768]{0:T(1024)}, u32[]{:S(2)}) copy-start(f32[768]{0:T(1024)} %get-tuple-element.22) | copy-start | bytes 9220
  302.4 138.4 %copy-start = (f32[3,128,768]{2,1,0:T(8,128)}, f32[3,128,768]{2,1,0:T(8,128)S(1)}, u32[]{:S(2)}) copy-start(f32[3,128,768]{2,1,0:T(8,128)S(1)} %get-tuple-element.40) | copy-start | bytes 3538948
  302.7 135.3 %copy-start.38 = (f32[3,128]{1,0:T(4,128)}, f32[3,128]{1,0:T(4,128)S(1)}, u32[]{:S(2)}) copy-start(f32[3,128]{1,0:T(4,128)S(1)} %add_rsqrt_fusion) | copy-start | bytes 4612
  365.7 65.3 %copy-start.17 = (bf16[3,128,768]{2,1,0:T(8,128)(2,1)S(1)}, bf16[3,128,768]{2,1,0:T(8,128)(2,1)}, u32[]{:S(2)}) copy-start(bf16[3,128,768]{2,1,0:T(8,128)(2,1)} %param.27) | copy-start | bytes 1769476
  443.9 195.6 %reduce-scatter.13.cloned.1.call-start = ((), (), s32[]{:S(2)}) async-start(), calls=%async_computation.17 | async-start | bytes 1216512 | tf_op jit(solution)/shard_map/reduce_scatter | solution.py:135
  460.9 278.9 %reduce-scatter.11.cloned.1.call-start = ((), (), s32[]{:S(2)}) async-start(), calls=%async_computation.16 | async-start | bytes 1216512 | tf_op jit(solution)/shard_map/reduce_scatter | solution.py:135
  466.8 376.2 %reduce-scatter.15.cloned.1.call-start = ((), (), s32[]{:S(2)}) async-start(), calls=%async_computation.18 | async-start | bytes 2433024 | tf_op jit(solution)/shard_map/reduce_scatter | solution.py:135
  485.1 466.3 %reduce-scatter.9.cloned.1.call-start = ((), (), s32[]{:S(2)}) async-start(), calls=%async_computation.15 | async-start | bytes 3649536 | tf_op jit(solution)/shard_map/reduce_scatter | solution.py:135
  509.1 554.6 %reduce-scatter.19.cloned.1.call-start = ((), (), s32[]{:S(2)}) async-start(), calls=%async_computation.20 | async-start | bytes 4866048 | tf_op jit(solution)/shard_map/reduce_scatter | solution.py:135
  516.6 658.5 %reduce-scatter.21.cloned.1.call-start = ((), (), s32[]{:S(2)}) async-start(), calls=%async_computation.21 | async-start | bytes 4866048 | tf_op jit(solution)/shard_map/reduce_scatter | solution.py:135
  533.3 67.6 %all-to-all-start = ((bf16[3,196,768]{1,0,2:T(4,128)(2,1)}), bf16[3,196,768]{1,0,2:T(4,128)(2,1)}, u32[]{:S(2)}, u32[]{:S(2)}) async-start(bf16[3,196,768]{1,0,2:T(4,128)(2,1)} %copy.164), calls=%async_computation | async-start | bytes 3145728 | tf_op jit(solution)/shard_map/all_to_all | solution.py:132
  (39 other events, 215.1 us)
Sparse Core Ops, SparseCore 0:
  10.9 59.9 all-gather.12
  73.9 59.0 all-gather.8
  135.8 52.8 all-gather.10
  191.5 53.0 all-gather.14
  247.3 53.0 all-gather.16
  303.1 62.5 all-gather.18
  368.6 62.3 all-gather.20
  444.0 95.0 reduce-scatter.16
  544.2 95.2 reduce-scatter.12
  644.4 95.2 reduce-scatter.10
  745.0 98.0 reduce-scatter.14
  849.2 102.1 reduce-scatter.8
  957.8 105.8 reduce-scatter.18
  1069.0 106.0 reduce-scatter.20

commit v2 on v1

--- a/solution.py
+++ b/solution.py
@@ -1,6 +1,10 @@
+import functools
+
 import jax
 import jax.numpy as jnp
 from jax import lax
+from jax.experimental import pallas as pl
+from jax.experimental.pallas import tpu as pltpu
 from jax.sharding import PartitionSpec as P
 
 HEADS = 12
@@ -9,6 +13,285 @@
 BOTH = ("dp", "seq")
 f32 = jnp.float32
 bf16 = jnp.bfloat16
+MESH = pl.DeviceIdType.MESH
+HBM = pltpu.MemorySpace.HBM
+VMEM = pltpu.MemorySpace.VMEM
+LANES = 128
+
+
+class Place:
+    def __init__(self, nz):
+        dp, seq = lax.axis_index("dp"), lax.axis_index("seq")
+        self.nz = nz
+        self.z, self.x = dp // 2, lax.rem(dp, 2)
+        self.y, self.c = seq // 2, lax.rem(seq, 2)
+        c, x, y = self.c, self.x, self.y
+        self.p = x + c * (y - x)
+        self.s = y + c * (x - y)
+        self.sib = (dp, 2 * y + (1 - c))
+        self.p_xy = (x + (1 - c) * (1 - 2 * x), y + c * (1 - 2 * y))
+        self.s_xy = (x + c * (1 - 2 * x), y + (1 - c) * (1 - 2 * y))
+        self.ps_xy = (1 - x, 1 - y)
+        self.p_dev = self.dev(self.z, self.p_xy)
+        self.s_dev = self.dev(self.z, self.s_xy)
+        self.z_of = [lax.rem(self.z + k, nz) for k in range(nz)]
+        self.z_devs = [self.dev(self.z_of[k], (x, y)) for k in range(nz)]
+
+    def dev(self, z, xy):
+        return (2 * z + xy[0], 2 * xy[1] + self.c)
+
+    def column(self, p, s):
+        return p + self.c * (s - p), s + self.c * (p - s)
+
+    def partners(self):
+        return [*self.z_devs[1:], self.p_dev, self.s_dev, self.sib]
+
+
+def enter(partners):
+    barrier = pltpu.get_barrier_semaphore()
+    for d in partners:
+        pl.semaphore_signal(barrier, inc=1, device_id=d, device_id_type=MESH)
+    pl.semaphore_wait(barrier, len(partners))
+
+
+def remote(src, dst, sems, i, dev):
+    return pltpu.make_async_remote_copy(
+        src_ref=src, dst_ref=dst, send_sem=sems[0].at[i], recv_sem=sems[1].at[i],
+        device_id=dev, device_id_type=MESH,
+    )
+
+
+class Gather:
+    def __init__(self, here, shard, full, sems, local):
+        h = here
+        x, y, c = h.x, h.y, h.c
+        mine = full.at[h.z, x, y, c]
+
+        def col(xy):
+            return full.at[:, xy[0], xy[1], c]
+
+        self.own = pltpu.make_async_copy(shard, mine, local)
+        nz = h.nz
+        self.zs = [remote(shard, mine, sems, k - 1, h.z_devs[k]) for k in range(1, nz)]
+        own, px, sx, psx = (x, y), h.p_xy, h.s_xy, h.ps_xy
+        n = nz - 1
+        self.p_own = remote(col(own), col(own), sems, n, h.p_dev)
+        self.s_own = remote(col(own), col(own), sems, n + 1, h.s_dev)
+        self.s_p = remote(col(px), col(px), sems, n + 2, h.s_dev)
+        self.sibs = [
+            remote(col(xy), col(xy), sems, n + 3 + i, h.sib)
+            for i, xy in enumerate((own, px, sx, psx))
+        ]
+
+    @staticmethod
+    def count(nz):
+        return nz + 6
+
+    def step(self, i):
+        if i == 0:
+            self.own.start()
+            for t in self.zs:
+                t.start()
+        elif i == 1:
+            self.own.wait()
+            for t in self.zs:
+                t.wait_recv()
+            self.p_own.start()
+            self.s_own.start()
+            self.sibs[0].start()
+        elif i == 2:
+            self.p_own.wait_recv()
+            self.s_p.start()
+            self.sibs[1].start()
+        elif i == 3:
+            self.s_own.wait_recv()
+            self.sibs[2].start()
+            self.s_p.wait_recv()
+            self.sibs[3].start()
+        elif i == 4:
+            for t in self.sibs:
+                t.wait_recv()
+        elif i == 5:
+            for t in (*self.zs, self.p_own, self.s_own, self.s_p, *self.sibs):
+                t.wait_send()
+
+
+def gather_kernel(nz, n_w, *refs):
+    shards, fulls = refs[:n_w], refs[n_w : 2 * n_w]
+    local, ssem, rsem = refs[2 * n_w :]
+    here = Place(nz)
+    enter(here.partners())
+    gs = [
+        Gather(here, shards[i], fulls[i], (ssem.at[i], rsem.at[i]), local.at[i]) for i in range(n_w)
+    ]
+    for g in gs:
+        g.step(0)
+    for t in range(n_w + 3):
+        for step in (4, 3, 2, 1):
+            i = t - (step - 1)
+            if 0 <= i < n_w:
+                gs[i].step(step)
+    for g in gs:
+        g.step(5)
+
+
+def gather_all(nz, shards):
+    n_w = len(shards)
+    count = Gather.count(nz)
+    outs = [jax.ShapeDtypeStruct((nz, 2, 2, 2, *w.shape), w.dtype) for w in shards]
+    return pl.pallas_call(
+        functools.partial(gather_kernel, nz, n_w),
+        out_shape=outs,
+        in_specs=[pl.BlockSpec(memory_space=HBM)] * n_w,
+        out_specs=[pl.BlockSpec(memory_space=HBM)] * n_w,
+        scratch_shapes=[
+            pltpu.SemaphoreType.DMA((n_w,)),
+            pltpu.SemaphoreType.DMA((n_w, count)),
+            pltpu.SemaphoreType.DMA((n_w, count)),
+        ],
+        compiler_params=pltpu.CompilerParams(collective_id=0, has_side_effects=True),
+    )(*shards)
+
+
+class Scatter:
+    def __init__(self, here, part, bufs, out, sems, local):
+        self.h, self.part, self.out = here, part, out
+        self.own, self.rc, self.rs, self.rp, self.rz = bufs
+        h = here
+        nz = h.nz
+        c = h.c
+        self.load = pltpu.make_async_copy(part.at[:, :, :, c], self.own, local)
+        self.core = remote(part.at[:, :, :, 1 - c], self.rc, sems, 0, h.sib)
+        self.s = [
+            remote(self.rc.at[:, *h.column(p, 1 - h.s)], self.rs.at[p], sems, 1 + i, h.s_dev)
+            for i, p in enumerate((1 - h.p, h.p))
+        ]
+        self.pp = remote(self.rs.at[1 - h.p], self.rp, sems, 3, h.p_dev)
+        self.zs = [
+            remote(self.rp.at[h.z_of[k]], self.rz.at[k - 1], sems, 3 + k, h.z_devs[k])
+            for k in range(1, nz)
+        ]
+
+    @staticmethod
+    def count(nz):
+        return nz + 3
+
+    def add(self, dst, a, b):
+        def body(z, _):
+            dst[z] = (a[z].astype(f32) + b[z].astype(f32)).astype(bf16)
+            return 0
+
+        lax.fori_loop(0, self.h.nz, body, 0)
+
+    def step(self, i):
+        h = self.h
+        if i == 0:
+            self.load.start()
+            self.core.start()
+        elif i == 1:
+            self.load.wait()
+            self.core.wait_recv()
+            for j, p in enumerate((1 - h.p, h.p)):
+                xy = h.column(p, 1 - h.s)
+                self.add(self.rc.at[:, *xy], self.rc.at[:, *xy], self.own.at[:, *xy])
+                self.s[j].start()
+            for p in (1 - h.p, h.p):
+                xy = h.column(p, h.s)
+                self.add(self.rc.at[:, *xy], self.rc.at[:, *xy], self.own.at[:, *xy])
+        elif i == 2:
+            xy = h.column(1 - h.p, h.s)
+            self.s[0].wait_recv()
+            self.add(self.rs.at[1 - h.p], self.rs.at[1 - h.p], self.rc.at[:, *xy])
+            self.pp.start()
+            xy = h.column(h.p, h.s)
+            self.s[1].wait_recv()
+            self.add(self.rs.at[h.p], self.rs.at[h.p], self.rc.at[:, *xy])
+        elif i == 3:
+            self.pp.wait_recv()
+            self.add(self.rp, self.rp, self.rs.at[h.p])
+            for t in self.zs:
+                t.start()
+        elif i == 4:
+            for t in self.zs:
+                t.wait_recv()
+            total = self.rp[h.z].astype(f32)
+            for k in range(h.nz - 1):
+                total = total + self.rz[k].astype(f32)
+            self.out[...] = total
+        elif i == 5:
+            for t in (self.core, *self.s, self.pp, *self.zs):
+                t.wait_send()
+
+
+def scatter_kernel(nz, n_w, *refs):
+    parts, img = refs[:n_w], refs[n_w]
+    outs, img_out = refs[n_w + 1 : 2 * n_w + 1], refs[2 * n_w + 1]
+    rest = refs[2 * n_w + 2 :]
+    bufs = [rest[5 * i : 5 * i + 5] for i in range(n_w)]
+    local, ssem, rsem, isem, jsem = rest[5 * n_w :]
+    here = Place(nz)
+    dp, seq = lax.axis_index("dp"), lax.axis_index("seq")
+    peers = [(dp, lax.rem(seq + k, 4)) for k in range(1, 4)]
+    enter([*here.partners(), *peers])
+    keep = pltpu.make_async_copy(img.at[seq], img_out.at[seq], local.at[n_w])
+    keep.start()
+    moves = [
+        remote(img.at[lax.rem(seq + k, 4)], img_out.at[seq], (isem, jsem), k - 1, peers[k - 1])
+        for k in range(1, 4)
+    ]
+    ss = [
+        Scatter(here, parts[i], bufs[i], outs[i], (ssem.at[i], rsem.at[i]), local.at[i])
+        for i in range(n_w)
+    ]
+    for s in ss:
+        s.step(0)
+    for m in moves:
+        m.start()
+    for t in range(n_w + 3):
+        for step in (4, 3, 2, 1):
+            i = t - (step - 1)
+            if 0 <= i < n_w:
+                ss[i].step(step)
+    for s in ss:
+        s.step(5)
+    keep.wait()
+    for m in moves:
+        m.wait()
+
+
+def scatter_all(nz, parts, img):
+    n_w = len(parts)
+    count = Scatter.count(nz)
+    scratch = []
+    for w in parts:
+        blk = w.shape[4:]
+        scratch += [
+            pltpu.VMEM((nz, 2, 2, *blk), bf16),
+            pltpu.VMEM((nz, 2, 2, *blk), bf16),
+            pltpu.VMEM((2, nz, *blk), bf16),
+            pltpu.VMEM((nz, *blk), bf16),
+            pltpu.VMEM((nz - 1, *blk), bf16),
+        ]
+    return pl.pallas_call(
+        functools.partial(scatter_kernel, nz, n_w),
+        out_shape=[
+            *(jax.ShapeDtypeStruct(w.shape[4:], f32) for w in parts),
+            jax.ShapeDtypeStruct(img.shape, img.dtype),
+        ],
+        in_specs=[pl.BlockSpec(memory_space=HBM)] * (n_w + 1),
+        out_specs=[*([pl.BlockSpec(memory_space=VMEM)] * n_w), pl.BlockSpec(memory_space=HBM)],
+        scratch_shapes=[
+            *scratch,
+            pltpu.SemaphoreType.DMA((n_w + 1,)),
+            pltpu.SemaphoreType.DMA((n_w, count)),
+            pltpu.SemaphoreType.DMA((n_w, count)),
+            pltpu.SemaphoreType.DMA((3,)),
+            pltpu.SemaphoreType.DMA((3,)),
+        ],
+        compiler_params=pltpu.CompilerParams(
+            collective_id=1, has_side_effects=True, vmem_limit_bytes=56 << 20
+        ),
+    )(*parts, img)
 
 
 def norm_stats(v):
@@ -120,22 +403,41 @@
 
 def on_device(captions, images, tissue_mask, gain_self, gain_cross, gain_mlp, *rest):
     weights, cotangent = rest[:-1], rest[-1]
+    n_dp, n_seq = lax.axis_size("dp"), lax.axis_size("seq")
     count = captions.shape[0]
     start = lax.axis_index("seq") * count
     img = lax.dynamic_slice_in_dim(images, start, count, 0)
     mask = lax.dynamic_slice_in_dim(tissue_mask, start, count, 0)
     gains = jnp.stack([gain_self, gain_cross, gain_mlp], axis=1)
-    gains = lax.all_gather(gains, BOTH, axis=0, tiled=True)
+    own_kernels = n_seq == 4 and n_dp % 2 == 0 and all(w.shape[0] % 8 == 0 for w in weights)
+    d = captions.shape[-1]
+    if own_kernels:
+        nz = n_dp // 2
+        pad = jnp.pad(gains, ((0, 0), (0, LANES - 3)))
+        *full, gains = gather_all(nz, [*weights, pad])
+        full = [w.reshape(-1, w.shape[-1]) for w in full]
+        gains = gains.reshape(-1, LANES)
+    else:
+        full = [lax.all_gather(w, BOTH, axis=0, tiled=True) for w in weights]
+        gains = lax.all_gather(gains, BOTH, axis=0, tiled=True)
     gains = tuple(gains[:, i] for i in range(3))
-    full = [lax.all_gather(w, BOTH, axis=0, tiled=True) for w in weights]
     out, gx0, gimg, gg, gw = layer(captions, img, mask, gains, full, cotangent)
-    gimg = lax.all_to_all(gimg, "seq", split_axis=2, concat_axis=0, tiled=True).astype(f32)
-    gg = lax.psum_scatter(jnp.stack(gg, axis=1), BOTH, scatter_dimension=0, tiled=True)
-    shards = [
-        lax.psum_scatter(g.astype(bf16), BOTH, scatter_dimension=0, tiled=True).astype(f32)
-        for g in gw
-    ]
-    return (out, gx0, gimg, gg[:, 0], gg[:, 1], gg[:, 2], *shards)
+    gg = jnp.stack(gg, axis=1)
+    gw = [g.astype(bf16) for g in gw]
+    if own_kernels:
+        pad = jnp.pad(gg, ((0, 0), (0, LANES - 3))).astype(bf16)
+        parts = [g.reshape(nz, 2, 2, 2, -1, g.shape[-1]) for g in (*gw[::-1], pad)]
+        img_parts = gimg.reshape(-1, n_seq, d // n_seq).swapaxes(0, 1)
+        *shards, gg, gimg = scatter_all(nz, parts, img_parts)
+        shards = shards[::-1]
+        gimg = gimg.reshape(images.shape[0], images.shape[1], -1)
+    else:
+        shards = [
+            lax.psum_scatter(g, BOTH, scatter_dimension=0, tiled=True).astype(f32) for g in gw
+        ]
+        gg = lax.psum_scatter(gg, BOTH, scatter_dimension=0, tiled=True)
+        gimg = lax.all_to_all(gimg, "seq", split_axis=2, concat_axis=0, tiled=True)
+    return (out, gx0, gimg.astype(f32), gg[:, 0], gg[:, 1], gg[:, 2], *shards)
 
 
 def solution(mesh):

time: 1190 us -> 394 us (0.33)
  waiting for transfers between devices: 890 us -> 0 us
  Pallas kernels: 0 us -> 232 us
  blocking collectives: 90.6 us -> 0 us
  matrix products: 129 us -> 110 us
  other arithmetic: 22.9 us -> 8.32 us
  between operations: 14.7 us -> 1.65 us
    reduce_scatter x7 -> x0, waiting for transfers between devices: 558 us -> none  [on_device(): lax.psum_scatter(g.astype(bf16), BOTH, scatter_dimension=0, tiled=True)]
    all_gather x7 -> x0, waiting for transfers between devices: 327 us -> none  [on_device(): full = [lax.all_gather(w, BOTH, axis=0, tiled=True) for w in weights]]
    pallas_call x0 -> x2, Pallas kernels: none -> 232 us  [the longest x1 129 us: scatter_all(): pl.pallas_call(functools.partial(scatter_kernel, nz, n_w), out_shape=[*(j...]
    unnamed x1 -> x0, blocking collectives: 47.4 us -> none
    all_gather x1 -> x0, blocking collectives: 43.3 us -> none  [on_device(): gains = lax.all_gather(gains, BOTH, axis=0, tiled=True)]
  transfers between devices with their start and end apart: 15 -> 0, of which waited for: 13 -> 0; matrix products, arithmetic and copies ran while one was open for 14% -> 0% of each run, Pallas kernels for 0% -> 0%
where the time goes in v2:
time: 394 us; the launch traced here: 388 us
  Pallas kernels  232 us (59%)
  matrix products  110 us (28%)
  local copies, waits for them, and re-layouts  36.1 us (9%)
  other arithmetic  8.32 us (2%)
    pallas_call x1, Pallas kernels, scatter_all(): pl.pallas_call(functools.partial(scatter_kernel, nz, n_w), out_shape=[*(j...  129 us
    pallas_call x1, Pallas kernels, gather_all(): pl.pallas_call(functools.partial(gather_kernel, nz, n_w), out_shape=outs,...  103 us
    dot_general x7, matrix products, wgrad(): return jnp.einsum('btd,bte->de', a, b, preferred_element_type=f32)  25.7 us
    dot_general x7, matrix products, mm_t(): return jnp.einsum('bte,de->btd', a, b, preferred_element_type=f32)  18.2 us
    dot_general x7, matrix products, mm(): return jnp.einsum('btd,de->bte', a, b, preferred_element_type=f32)  16.8 us
    dot_general x2, matrix products, attend_back(): jnp.einsum('bhqk,bkhe->bqhe', ds, k, preferred_element_type=f32)  13.3 us
    dot_general x2, matrix products, attend_back(): jnp.einsum('bhqk,bqhe->bkhe', ds, q, preferred_element_type=f32)  11.5 us
    sub x2, matrix products, attend(): ex = jnp.exp(s - jnp.max(s, axis=-1, keepdims=True))  9.08 us

profile of v2, /device:TPU:0, one launch (start us, length us, event | category | flops | bytes accessed | tf_op | source)
XLA Modules:
  0.0 388.4 jit_solution(18424606733614736899)
XLA Ops:
  6.1 103.3 %shard_map.237 = (bf16[4,2,2,2,24,2304]{5,4,3,2,1,0:T(8,128)(2,1)}, bf16[4,2,2,2,24,768]{5,4,3,2,1,0:T(8,128)(2,1)}, bf16[4,2,2,2,24,768]{5,4,3,2,1,0:T(8,128)(2...) custom-call(bf16[24,2304]{1,0:T(8,128)(2,1)} %refs_0_.1, ...), custom_call_target="tpu_custom_call" | custom-call | tf_op jit(solution)/shard_map/pallas_call | solution.py:142
  111.8 3.6 convolution_convert_fusion
  118.0 3.8 convolution_convert_fusion.1
  124.2 4.0 %fusion.105 = (f32[3,12,128]{2,1,0:T(8,128)S(1)}, f32[3,12,128,128]{2,3,1,0:T(8,128)}) fusion(pred[128,128]{0,1:T(8,128)(4,1)S(1)} %copy-done.35, bf16[3,128,12,64]{1,3,2,0:T(8,128)(2,1)} %bitcast.160, bf16[3,128,12,64]{1,3,2,0:T(8,128)(2,1)} %bitcast.158), kind=kOutput, calls=%fused_computation.156 | convolution fusion | flops 77856896 | bytes 3573760 | tf_op jit(solution)/shard_map/sub | solution.py:331
  133.1 5.1 %fusion.107 = (f32[3,12,128]{2,1,0:T(8,128)S(1)}, f32[3,12,128,196]{2,3,1,0:T(8,128)}) fusion(pred[3,196]{1,0:T(4,128)(4,1)S(1)} %dynamic-slice_compare_fusion, bf16[3,128,12,64]{1,3,2,0:T(8,128)(2,1)S(1)} %bitcast.162, bf16[3,196,12,64]{1,3,2,0:T(8,128)(2,1)} %bitcast.153), kind=kOutput, calls=%fused_computation.158 | convolution fusion | flops 119218368 | bytes 5124684 | tf_op jit(solution)/shard_map/sub | solution.py:331
  138.2 3.0 convolution_convert_fusion.7
  143.1 4.4 %multiply_convert_fusion = (bf16[3,128,3072]{2,1,0:T(8,128)(2,1)S(1)}, f32[3,128,3072]{2,1,0:T(8,128)S(1)}) fusion(bf16[768,3072,1]{1,0,2:T(8,128)(2,1)} %bitcast.172, f32[3,128,768]{2,1,0:T(8,128)S(1)} %get-tuple-element.113, f32[768]{0:T(1024)S(1)} %copy-done.33, f32[3,128]{1,0:T(4,128)S(1)} %add_rsqrt_fusion, f32[3,128]{1,0:T(4,128)S(1)} %broadcast_multiply_fusion.6), kind=kOutput, calls=%fused_computation.15 | convolution fusion | flops 1819017216 | bytes 12982272 | tf_op jit(solution)/shard_map/btd,de->bte/dot_general | solution.py:312
  147.6 3.7 fusion.9
  151.3 2.8 fusion.44
  161.1 3.0 bitcast_convert_fusion.6
  164.2 4.7 %bitcast_convert_fusion = bf16[768,3072]{1,0:T(8,128)(2,1)} fusion(bf16[3,128,3072]{2,1,0:T(8,128)(2,1)S(1)} %copy-done.45, f32[3,128,768]{2,1,0:T(8,128)S(1)} %get-tuple-element.113, f32[768]{0:T(1024)S(1)} %copy-done.34, f32[3,128]{1,0:T(4,128)S(1)} %copy-done.41, f32[3,128]{1,0:T(4,128)S(1)} %broadcast_multiply_fusion.6), kind=kOutput, calls=%fused_computation.4 | convolution fusion | flops 1815478272 | bytes 8263680 | tf_op jit(solution)/shard_map/btd,bte->de/dot_general | solution.py:320
  173.7 4.1 %fusion.109 = f32[3,12,128,196]{2,3,1,0:T(8,128)} fusion(bf16[3,128,12,64]{1,3,2,0:T(8,128)(2,1)} %bitcast.148, bf16[3,196,12,64]{1,3,2,0:T(8,128)(2,1)S(1)} %bitcast.139), kind=kOutput, calls=%fused_computation.160 | convolution fusion | flops 115605504 | bytes 5105664 | tf_op jit(solution)/shard_map/bqhe,bkhe->bhqk/dot_general | solution.py:338
  177.7 7.9 %fusion.45 = bf16[3,12,64,128]{3,2,1,0:T(8,128)(2,1)} fusion(bf16[3,196,12,64]{1,3,2,0:T(8,128)(2,1)} %bitcast.154, f32[3,12,128,196]{2,3,1,0:T(8,128)} %fusion.109, f32[3,12,128,196]{2,3,1,0:T(8,128)} %get-tuple-element.111, f32[3,12,128]{2,1,0:T(8,128)} %copy-done.52), kind=kOutput, calls=%fused_computation.61 | convolution fusion | flops 122227392 | bytes 8736768 | tf_op jit(solution)/shard_map/bhqk,bkhe->bqhe/dot_general | solution.py:340
  185.6 6.9 %fusion.35 = bf16[3,12,64,196]{3,2,1,0:T(8,128)(2,1)S(1)} fusion(bf16[3,128,12,64]{1,3,2,0:T(8,128)(2,1)} %bitcast.163, f32[3,12,128,196]{2,3,1,0:T(8,128)} %fusion.109, f32[3,12,128,196]{2,3,1,0:T(8,128)} %get-tuple-element.111, f32[3,12,128]{2,1,0:T(8,128)} %copy-done.52), kind=kOutput, calls=%fused_computation.49 | convolution fusion | flops 122384064 | bytes 8736768 | tf_op jit(solution)/shard_map/bhqk,bqhe->bkhe/dot_general | solution.py:341
  194.0 4.9 %convolution_convert_fusion.3 = bf16[3,196,768]{2,1,0:T(8,128)(2,1)} fusion(bf16[768,1536,1]{1,0,2:T(8,128)(2,1)} %bitcast.183, bf16[3,196,768]{2,1,0:T(8,128)(2,1)} %copy.126, bf16[3,196,768]{2,1,0:T(8,128)(2,1)} %copy.125), kind=kOutput, calls=%fused_computation.51 | convolution fusion | flops 1391330304 | bytes 5068800 | tf_op jit(solution)/shard_map/bte,de->btd/dot_general | solution.py:316
  203.6 3.8 reshape.260
  207.4 2.6 copy.151
  209.9 4.8 %bitcast_convert_fusion.3 = bf16[768,1536]{1,0:T(8,128)(2,1)} fusion(bf16[3,196,768]{2,1,0:T(8,128)(2,1)S(1)} %copy-done.13, bf16[3,196,768]{2,1,0:T(8,128)(2,1)S(1)} %copy-done.14, bf16[12,196,768]{2,1,0:T(8,128)(2,1)} %param.15, s32[]{:T(128)S(6)} %select_n.13), kind=kOutput, calls=%fused_computation.14 | convolution fusion | flops 1392058368 | bytes 5087236 | tf_op jit(solution)/shard_map/btd,bte->de/dot_general | solution.py:320
  221.7 5.5 %fusion.48 = bf16[3,12,64,128]{3,2,1,0:T(8,128)(2,1)} fusion(bf16[3,128,12,64]{1,3,2,0:T(8,128)(2,1)S(1)} %bitcast.159, f32[3,12,128,128]{2,3,1,0:T(8,128)} %fusion.110, f32[3,12,128,128]{2,3,1,0:T(8,128)} %get-tuple-element.107, f32[3,12,128]{2,1,0:T(8,128)} %copy-done.50), kind=kOutput, calls=%fused_computation.68 | convolution fusion | flops 79925888 | bytes 5916672 | tf_op jit(solution)/shard_map/bhqk,bkhe->bqhe/dot_general | solution.py:340
  227.1 4.6 %fusion.51 = bf16[3,12,64,128]{3,2,1,0:T(8,128)(2,1)S(1)} fusion(bf16[3,128,12,64]{1,3,2,0:T(8,128)(2,1)S(1)} %bitcast.161, f32[3,12,128,128]{2,3,1,0:T(8,128)} %fusion.110, f32[3,12,128,128]{2,3,1,0:T(8,128)} %get-tuple-element.107, f32[3,12,128]{2,1,0:T(8,128)} %copy-done.50), kind=kOutput, calls=%fused_computation.69 | convolution fusion | flops 79925888 | bytes 5916672 | tf_op jit(solution)/shard_map/bhqk,bqhe->bkhe/dot_general | solution.py:341
  233.4 4.0 %fusion.59 = (bf16[768]{0:T(1024)(128)(2,1)S(1)}, f32[3,128]{1,0:T(4,128)S(1)}, f32[3,128]{1,0:T(4,128)S(1)}, f32[3,128,768]{2,1,0:T(8,128)S(1)}) fusion(bf16[3,128,768]{2,1,0:T(8,128)(2,1)S(1)} %copy-done.1, f32[3,128]{1,0:T(4,128)} %copy-done.37, f32[3,128]{1,0:T(4,128)S(1)} %broadcast_multiply_fusion.8, f32[768]{0:T(1024)S(1)} %copy-done.32, ...), kind=kOutput, calls=%fused_computation.76 | convolution fusion | flops 1366915584 | bytes 7088640 | tf_op jit(solution)/shard_map/bte,de->btd/dot_general | solution.py:316
  239.8 5.1 %bitcast_convert_fusion.2 = bf16[768,2304]{1,0:T(8,128)(2,1)} fusion(bf16[3,128,768]{2,1,0:T(8,128)(2,1)S(1)} %copy.122, bf16[3,128,768]{2,1,0:T(8,128)(2,1)S(1)} %copy.121, bf16[3,128,768]{2,1,0:T(8,128)(2,1)} %copy-done.20, bf16[3,128,768]{2,1,0:T(8,128)(2,1)S(1)} %copy-done.1, f32[768]{0:T(1024)S(1)} %copy-done.32, f32[3,128]{1,0:T(4,128)S(1)} %copy-done.39, ...), kind=kOutput, calls=%fused_computation.6 | convolution fusion | flops 1367506944 | bytes 5904384 | tf_op jit(solution)/shard_map/btd,bte->de/dot_general | solution.py:320
  245.0 4.3 %bitcast_convert_fusion.1 = bf16[3072,768]{1,0:T(8,128)(2,1)} fusion(bf16[3,128,3072]{2,1,0:T(8,128)(2,1)S(1)} %copy-done.49, bf16[3,128,768]{2,1,0:T(8,128)(2,1)S(1)} %copy-done.16), kind=kOutput, calls=%fused_computation.5 | convolution fusion | flops 1814298624 | bytes 7667712 | tf_op jit(solution)/shard_map/btd,bte->de/dot_general | solution.py:320
  249.3 129.1 %shard_map.238 = (f32[96,768]{1,0:T(8,128)}, f32[24,3072]{1,0:T(8,128)}, f32[24,768]{1,0:T(8,128)}, f32[24,1536]{1,0:T(8,128)}, f32[24,768]{1,0:T(8,128)}, /*ind...) custom-call(bf16[4,2,2,2,96,768]{5,4,3,2,1,0:T(8,128)(2,1)} %bitcast.130, ...), custom_call_target="tpu_custom_call" | custom-call | tf_op jit(solution)/shard_map/pallas_call | solution.py:275
  (192 shorter events, 58.0 us)
Async XLA Ops:
  0.6 111.1 %copy-start = (bf16[3,128,768]{2,1,0:T(8,128)(2,1)S(1)}, bf16[3,128,768]{2,1,0:T(8,128)(2,1)}, u32[]{:S(2)}) copy-start(bf16[3,128,768]{2,1,0:T(8,128)(2,1)} %param.14) | copy-start | bytes 1769476
  4.8 107.0 %copy-start.37 = (f32[3,128]{1,0:T(4,128)}, f32[3,128]{1,0:T(4,128)S(1)}, u32[]{:S(2)}) copy-start(f32[3,128]{1,0:T(4,128)S(1)} %add_rsqrt_fusion.2) | copy-start | bytes 4612
  118.0 10.2 %copy-start.8 = (bf16[3,128,768]{1,2,0:T(8,128)(2,1)}, bf16[3,128,768]{1,2,0:T(8,128)(2,1)S(1)}, u32[]{:S(2)}) copy-start(bf16[3,128,768]{1,2,0:T(8,128)(2,1)S(1)} %copy.102) | copy-start | bytes 1769476
  124.2 14.0 %copy-start.5 = (bf16[3,196,768]{1,2,0:T(8,128)(2,1)}, bf16[3,196,768]{1,2,0:T(8,128)(2,1)S(1)}, u32[]{:S(2)}) copy-start(bf16[3,196,768]{1,2,0:T(8,128)(2,1)S(1)} %copy.107) | copy-start | bytes 2709508
  133.1 5.1 %copy-start.19 = (bf16[3,128,768]{1,2,0:T(8,128)(2,1)}, bf16[3,128,768]{1,2,0:T(8,128)(2,1)S(1)}, u32[]{:S(2)}) copy-start(bf16[3,128,768]{1,2,0:T(8,128)(2,1)S(1)} %copy.109) | copy-start | bytes 1769476
  142.7 4.8 %slice-start.2 = ((s8[4718592]{0:T(1024)(128)(4,1)}), s8[4194304]{0:T(1024)(128)(4,1)S(1)}, s32[]{:S(2)}) async-start(s8[4718592]{0:T(1024)(128)(4,1)} %bitcast.176), calls=%async_computation.2 | async-start | bytes 8388608
  143.0 14.0 %copy-start.40 = (f32[3,128]{1,0:T(4,128)}, f32[3,128]{1,0:T(4,128)S(1)}, u32[]{:S(2)}) copy-start(f32[3,128]{1,0:T(4,128)S(1)} %add_rsqrt_fusion) | copy-start | bytes 4612
  143.0 4.5 %copy-start.15 = (bf16[3,128,768]{2,1,0:T(8,128)(2,1)S(1)}, bf16[3,128,768]{2,1,0:T(8,128)(2,1)}, u32[]{:S(2)}) copy-start(bf16[3,128,768]{2,1,0:T(8,128)(2,1)} %param.27) | copy-start | bytes 1769476
  143.1 11.1 %slice-start = ((s8[4718592]{0:T(1024)(128)(4,1)}), s8[4194304]{0:T(1024)(128)(4,1)S(1)}, s32[]{:S(2)}) async-start(s8[4718592]{0:T(1024)(128)(4,1)} %bitcast.173), calls=%async_computation | async-start | bytes 8388608
  147.5 6.6 %slice-start.1 = ((s8[4718592]{0:T(1024)(128)(4,1)}), s8[524288]{0:T(1024)(128)(4,1)S(1)}, s32[]{:S(2)}) async-start(s8[4718592]{0:T(1024)(128)(4,1)} %bitcast.173), calls=%async_computation.1 | async-start | bytes 1048576
  164.2 4.7 %copy-start.10 = (bf16[3,128,768]{1,2,0:T(8,128)(2,1)S(1)}, bf16[3,128,768]{1,2,0:T(8,128)(2,1)}, u32[]{:S(2)}) copy-start(bf16[3,128,768]{1,2,0:T(8,128)(2,1)} %copy.114) | copy-start | bytes 1769476
  164.2 4.7 %copy-start.47 = (f32[3,12,128,196]{2,3,1,0:T(8,128)S(1)}, f32[3,12,128,196]{2,3,1,0:T(8,128)}, u32[]{:S(2)}) copy-start(f32[3,12,128,196]{2,3,1,0:T(8,128)} %get-tuple-element.111) | copy-start | bytes 10838020
  164.2 4.7 %copy-start.53 = (f32[3,12,128]{2,1,0:T(8,128)S(1)}, f32[3,12,128]{2,1,0:T(8,128)}, u32[]{:S(2)}) copy-start(f32[3,12,128]{2,1,0:T(8,128)} %copy-done.52) | copy-start | bytes 55300
  194.0 4.9 %copy-start.21 = (bf16[3,12,64,128]{3,2,1,0:T(8,128)(2,1)S(1)}, bf16[3,12,64,128]{3,2,1,0:T(8,128)(2,1)}, u32[]{:S(2)}) copy-start(bf16[3,12,64,128]{3,2,1,0:T(8,128)(2,1)} %fusion.45) | copy-start | bytes 1769476
  194.0 4.9 %copy-start.30 = (f32[3,128]{1,0:T(4,128)S(1)}, f32[3,128]{1,0:T(4,128)}, u32[]{:S(2)}) copy-start(f32[3,128]{1,0:T(4,128)} %copy-done.29) | copy-start | bytes 4612
  194.0 4.9 %copy-start.43 = (bf16[4,2,2,2,24,768]{5,4,3,2,1,0:T(8,128)(2,1)S(1)}, bf16[4,2,2,2,24,768]{5,4,3,2,1,0:T(8,128)(2,1)}, u32[]{:S(2)}) copy-start(bf16[4,2,2,2,24,768]{5,4,3,2,1,0:T(8,128)(2,1)} %get-tuple-element.34) | copy-start | bytes 3538948
  203.5 6.4 %copy-start.13 = (bf16[3,196,768]{2,1,0:T(8,128)(2,1)S(1)}, bf16[3,196,768]{2,1,0:T(8,128)(2,1)}, u32[]{:S(2)}) copy-start(bf16[3,196,768]{2,1,0:T(8,128)(2,1)} %copy.126) | copy-start | bytes 2709508
  209.9 4.8 %copy-start.46 = (f32[3,12,128,128]{2,3,1,0:T(8,128)S(1)}, f32[3,12,128,128]{2,3,1,0:T(8,128)}, u32[]{:S(2)}) copy-start(f32[3,12,128,128]{2,3,1,0:T(8,128)} %get-tuple-element.107) | copy-start | bytes 7077892
  209.9 4.8 %copy-start.51 = (f32[3,12,128]{2,1,0:T(8,128)S(1)}, f32[3,12,128]{2,1,0:T(8,128)}, u32[]{:S(2)}) copy-start(f32[3,12,128]{2,1,0:T(8,128)} %copy-done.50) | copy-start | bytes 55300
  221.6 5.5 %copy-start.18 = (bf16[3,128,768]{1,2,0:T(8,128)(2,1)S(1)}, bf16[3,128,768]{1,2,0:T(8,128)(2,1)}, u32[]{:S(2)}) copy-start(bf16[3,128,768]{1,2,0:T(8,128)(2,1)} %copy.103) | copy-start | bytes 1769476
  239.8 5.1 %copy-start.16 = (bf16[3,128,768]{2,1,0:T(8,128)(2,1)S(1)}, bf16[3,128,768]{2,1,0:T(8,128)(2,1)}, u32[]{:S(2)}) copy-start(bf16[3,128,768]{2,1,0:T(8,128)(2,1)} %param.27) | copy-start | bytes 1769476
  239.8 5.1 %copy-start.49 = (bf16[3,128,3072]{2,1,0:T(8,128)(2,1)S(1)}, bf16[3,128,3072]{2,1,0:T(8,128)(2,1)}, u32[]{:S(2)}) copy-start(bf16[3,128,3072]{2,1,0:T(8,128)(2,1)} %copy-done.48) | copy-start | bytes 7077892
  381.3 4.8 %copy-start.26 = (f32[24,768]{1,0:T(8,128)S(1)}, f32[24,768]{1,0:T(8,128)}, u32[]{:S(2)}) copy-start(f32[24,768]{1,0:T(8,128)} %get-tuple-element.144) | copy-start | bytes 221188
  381.4 5.4 %copy-start.23 = (f32[24,3072]{1,0:T(8,128)S(1)}, f32[24,3072]{1,0:T(8,128)}, u32[]{:S(2)}) copy-start(f32[24,3072]{1,0:T(8,128)} %get-tuple-element.145) | copy-start | bytes 884740
  (34 other events, 92.2 us)
